TPU v7x, 512 devices: a whole 4x8x8 slice. The times are simulated.
512 devices in a mesh: context: 32 (over y, x), tensor: 16 (over z, core).
Axes of the slice: x: 4, y: 8, z: 8, core: 2. Of those that a mesh axis runs over, the one named last changes fastest.
Arguments:
- queries: bfloat16 [1, 16384, 4096], P(None, 'context', 'tensor'), may hold values from -6 to 6
- keys: bfloat16 [1, 16384, 4096], P(None, 'context', 'tensor'), may hold values from -0.546875 to 0.546875
- spike_counts: int32 [1, 16384, 4096], P(None, 'context', 'tensor'), may hold values from -4 to 4
- spike_scale: float32 [4096], P('tensor'), may hold values from 0.5 to 2
- log_decay: float32 [1, 32, 16384], P(None, 'tensor', 'context'), may hold values from -3 to 0, as said below
- norm_gain: float32 [4096], P('tensor'), may hold values from 0.5 to 1.5
- out_weight: bfloat16 [4096, 8192], P('context', 'tensor'), may hold values from -0.09375 to 0.09375
- residual_in: bfloat16 [1, 16384, 8192], P(None, 'context', 'tensor'), may hold values from -6 to 6
Outputs:
- residual_out: bfloat16 [1, 16384, 8192], P(None, 'context', 'tensor')
Inputs may be any that keep to these rules, and one draw needn't show every extreme that they name: log_decay is negative.
All inputs are finite; a program needn't handle non-finite values.
Results may differ from a plain program's by a relative error of at most 0.0095.
Values may be sent and summed in bfloat16 or wider, within the bound.
A program may use at most 64 MiB of HBM per device.

v0:
```python
import jax
import jax.numpy as jnp
from jax import lax
from jax.sharding import PartitionSpec as P

epsilon = 1e-06


def prefix_2(value, axis, combine, identity):
    size, position = (lax.axis_size(axis), lax.axis_index(axis))
    everything = jax.tree.map(
        lambda part, kind: lax.all_gather(part.astype(kind), axis),
        value,
        (jnp.bfloat16, jnp.bfloat16),
    )
    start = jax.tree.map(
        lambda part, zero: jnp.broadcast_to(jnp.asarray(zero, part.dtype), part.shape),
        value,
        identity,
    )

    def lap(k, before):
        reached = k < position
        new = combine(
            before, jax.tree.map(lambda part, own: part[k].astype(own.dtype), everything, value)
        )
        return jax.tree.map(lambda a, b: jnp.where(reached, a, b), new, before)

    return lax.fori_loop(0, size, lap, start)


def combine(earlier, later):
    return (earlier[0] * later[0], later[0][..., None, None] * earlier[1] + later[1])


def local(queries, keys, spike_counts, spike_scale, log_decay, norm_gain, out_weight, residual_in):
    requests, block, width_here = queries.shape
    heads = log_decay.shape[1]
    head_size = width_here // heads
    values = (spike_counts.astype(jnp.float32) * spike_scale).astype(jnp.bfloat16)

    def split_heads(array):
        return array.reshape(requests, block, heads, head_size).transpose(0, 2, 1, 3)

    query_h = split_heads(queries)
    key_h = split_heads(keys)
    value_h = split_heads(values)
    cumulative = jnp.cumsum(log_decay, axis=2)
    vocabulary_identifiers = jnp.arange(block)
    causal = vocabulary_identifiers[:, None] >= vocabulary_identifiers[None, :]
    gaps = cumulative[..., :, None] - cumulative[..., None, :]
    decay_mat = jnp.exp(jnp.where(causal, gaps, -1e30))
    scores = jnp.einsum("rhtd,rhsd->rhts", query_h, key_h, preferred_element_type=jnp.float32)
    weights = (scores * decay_mat).astype(jnp.bfloat16)
    intra = jnp.einsum("rhts,rhsd->rhtd", weights, value_h, preferred_element_type=jnp.float32)
    to_end = jnp.exp(cumulative[..., -1:] - cumulative)
    weighted_keys = (key_h.astype(jnp.float32) * to_end[..., None]).astype(jnp.bfloat16)
    own_state = jnp.einsum(
        "rhsd,rhse->rhde", weighted_keys, value_h, preferred_element_type=jnp.float32
    )
    span_decay = jnp.exp(cumulative[..., -1])
    prefix = prefix_2(
        (span_decay, own_state),
        "context",
        combine,
        (jnp.ones_like(span_decay), jnp.zeros_like(own_state)),
    )
    incoming = prefix[1]
    carried = jnp.exp(cumulative)[..., None] * jnp.einsum(
        "rhtd,rhde->rhte", query_h.astype(jnp.float32), incoming, precision=lax.Precision.HIGHEST
    )
    mixed = intra + carried
    scale = lax.rsqrt(jnp.mean(mixed * mixed, axis=-1, keepdims=True) + epsilon)
    normed = (mixed * scale * norm_gain.reshape(1, heads, 1, head_size)).astype(jnp.bfloat16)
    normed = normed.transpose(0, 2, 1, 3).reshape(requests * block, width_here)
    all_heads = lax.all_gather(normed, "tensor", axis=1, tiled=True)
    projected = jnp.dot(
        all_heads,
        lax.all_gather(out_weight, "context", axis=0, tiled=True),
        preferred_element_type=jnp.float32,
    )
    projected = projected.reshape(requests, block, out_weight.shape[1])
    return (residual_in.astype(jnp.float32) + projected).astype(jnp.bfloat16)


def solution(mesh):
    in_specs = (
        P(None, "context", "tensor"),
        P(None, "context", "tensor"),
        P(None, "context", "tensor"),
        P("tensor"),
        P(None, "tensor", "context"),
        P("tensor"),
        P("context", "tensor"),
        P(None, "context", "tensor"),
    )
    out_specs = P(None, "context", "tensor")
    return jax.shard_map(local, mesh=mesh, in_specs=in_specs, out_specs=out_specs, check_vma=False)
```

profile of v0, /device:TPU:1, one launch (start us, length us, event | category | flops | bytes accessed | tf_op | source)
XLA Modules:
  0.0 247.4 jit_solution(11480079209673487597)
XLA Ops:
  8.4 1.1 copy.44
  9.5 1.1 multiply_convert_fusion.3
  12.7 31.4 %all-gather = bf16[32,2,1]{2,1,0:T(2,128)(2,1)S(1)} all-gather(bf16[1,2,1]{2,1,0:T(2,128)(2,1)S(1)} %get-tuple-element.154), channel_id=2, replica_groups=mesh['context'=32,'tensor'=16] {'context'}, dimensions={0}, use_global_device_ids=true | all-gather | bytes 132 | tf_op jit(solution)/shard_map/all_gather | solution.py:12
  44.3 52.7 %all-gather.10.cloned.1.call-done = bf16[64,128,128]{2,1,0:T(8,128)(2,1)} async-done(((bf16[2,128,128]{2,1,0:T(8,128)(2,1)}), bf16[64,128,128]{2,1,0:T(8,128)(2,1)}) %all-gather.10.cloned.1.call-update) | async-done | bytes 2097168 | tf_op jit(solution)/shard_map/all_gather | solution.py:12
  97.0 36.8 %while.14 = (s32[]{:T(128)}, f32[1,2,128,128]{3,2,1,0:T(8,128)S(1)}, s32[]{:T(128)}, bf16[32,1,2]{0,2,1:T(2,128)(2,1)S(1)}, bf16[32,1,2,128,128]{4,3,2,1,0:T(8,128)(2,1)}, /*index=5*/s32[]{:T(128)}, s32[]{:T(128)}) while((s32[]{:T(128)}, f32[1,2,128,128]{3,2,1,0:T(8,128)S(1)}, s32[]{:T(128)}, bf16[32,1,2]{0,2,1:T(2,128)(2,1)S(1)}, ...), condition=%wide.region_3.4_spmd.clone, body=%wide.region_2.3_spmd.clone.sunk | while | flops 163846 | bytes 327829 | solution.py:29
  98.3 0.9 fusion.25
  99.5 0.9 fusion.25
  100.6 0.9 fusion.25
  101.8 0.9 fusion.25
  102.9 0.9 fusion.25
  104.1 0.9 fusion.25
  105.2 0.9 fusion.25
  106.4 0.9 fusion.25
  107.5 0.9 fusion.25
  108.7 0.9 fusion.25
  109.8 0.9 fusion.25
  111.0 0.9 fusion.25
  112.1 0.9 fusion.25
  113.3 0.9 fusion.25
  114.4 0.9 fusion.25
  115.6 0.9 fusion.25
  116.7 0.9 fusion.25
  119.0 0.9 fusion.25
  121.3 0.9 fusion.25
  122.5 0.9 fusion.25
  124.8 0.9 fusion.25
  128.2 0.9 fusion.25
  130.5 0.9 fusion.25
  134.2 1.0 multiply_reduce_fusion
  136.1 49.7 %all-gather.8.cloned.1.call-done = bf16[4096,512]{1,0:T(8,128)(2,1)} async-done(((bf16[128,512]{1,0:T(8,128)(2,1)}), bf16[4096,512]{1,0:T(8,128)(2,1)}) %all-gather.8.cloned.1.call-update) | async-done | bytes 4194320 | tf_op jit(solution)/shard_map/all_gather | solution.py:79
  185.8 48.4 %all-gather.6.cloned.1.call-done = bf16[512,4096]{0,1:T(8,128)(2,1)} async-done(((bf16[512,256]{0,1:T(8,128)(2,1)}), bf16[512,4096]{0,1:T(8,128)(2,1)}) %all-gather.6.cloned.1.call-update) | async-done | bytes 4194320 | tf_op jit(solution)/shard_map/all_gather | solution.py:76
  234.3 6.6 %fusion.3 = bf16[1,512,512]{2,1,0:T(8,128)(2,1)} fusion(bf16[512,4096]{0,1:T(8,128)(2,1)} %all-gather.6.cloned.1.call-done, bf16[4096,512]{1,0:T(8,128)(2,1)} %all-gather.8.cloned.1.call-done, bf16[1,512,512]{2,1,0:T(8,128)(2,1)S(1)} %copy-done.2), kind=kOutput, calls=%fused_computation.8 | convolution fusion | flops 2148270080 | bytes 9437184 | tf_op jit(solution)/shard_map/dot_general | solution.py:77
  (140 shorter events, 19.9 us)
Async XLA Ops:
  6.5 37.7 %copy-start = (bf16[1,512,256]{2,1,0:T(8,128)(2,1)S(1)}, bf16[1,512,256]{2,1,0:T(8,128)(2,1)}, u32[]{:S(2)}) copy-start(bf16[1,512,256]{2,1,0:T(8,128)(2,1)} %param.10) | copy-start | bytes 786436
  6.5 90.4 %all-gather.10.cloned.1.call-start = ((), (), s32[]{:S(2)}) async-start(), calls=%async_computation.2 | async-start | bytes 2162688 | tf_op jit(solution)/shard_map/all_gather | solution.py:12
  11.8 174.0 %all-gather.8.cloned.1.call-start = ((), (), s32[]{:S(2)}) async-start(), calls=%async_computation.1 | async-start | bytes 4325376 | tf_op jit(solution)/shard_map/all_gather | solution.py:79
  12.6 221.7 %all-gather.6.cloned.1.call-start = ((), (), s32[]{:S(2)}) async-start(), calls=%async_computation | async-start | bytes 4456448 | tf_op jit(solution)/shard_map/all_gather | solution.py:76
  134.2 1.1 copy-start.1
  134.2 100.1 %copy-start.2 = (bf16[1,512,512]{2,1,0:T(8,128)(2,1)S(1)}, bf16[1,512,512]{2,1,0:T(8,128)(2,1)}, u32[]{:S(2)}) copy-start(bf16[1,512,512]{2,1,0:T(8,128)(2,1)} %param.17) | copy-start | bytes 1572868
Sparse Core Ops, SparseCore 0:
  11.9 85.0 all-gather.9
  100.1 85.6 all-gather.7
  187.9 46.2 all-gather.5
where the time goes:
time: 249 us; the launch traced here: 247 us
  waiting for transfers between devices  152 us (61%)
  other arithmetic  33 us (13%)
  blocking collectives  31.4 us (13%)
  between operations  13.2 us (5%)
  matrix products  8.93 us (4%)
  local copies, waits for them, and re-layouts  8.36 us (3%)
    all_gather x1, waiting for transfers between devices, prefix_2(): lax.all_gather(part.astype(kind), axis)  52.7 us
    all_gather x1, waiting for transfers between devices, local(): lax.all_gather(out_weight, 'context', axis=0, tiled=True)  49.7 us
    all_gather x1, waiting for transfers between devices, local(): all_heads = lax.all_gather(normed, 'tensor', axis=1, tiled=True)  48.4 us
    all_gather x1, blocking collectives, prefix_2(): lax.all_gather(part.astype(kind), axis)  31.4 us
    select_n x32, other arithmetic, lap(): return jax.tree.map(lambda a, b: jnp.where(reached, a, b), new, before)  29.7 us
    dot_general x1, matrix products, local(): jnp.dot(all_heads, lax.all_gather(out_weight, 'context', axis=0, tiled=Tr...  6.61 us
    dynamic_slice x64, local copies, waits for them, and re-layouts, lap(): part[k].astype(own.dtype)  6.03 us
  transfers between devices with their start and end apart: 3, of which 3 were waited for; matrix products, arithmetic and copies ran while one was open for 16% of the time, Pallas kernels for 0%

commit v1 on v0

--- a/solution.py
+++ b/solution.py
@@ -4,6 +4,19 @@
 from jax.sharding import PartitionSpec as P
 
 epsilon = 1e-06
+
+
+def gather_around(array, axis, dim):
+    ways = lax.axis_size(axis)
+    up = [(d, (d + 1) % ways) for d in range(ways)]
+    down = [(d, (d - 1) % ways) for d in range(ways)]
+    earlier, later = ([array], [array])
+    for _ in range(ways // 2):
+        earlier.append(lax.ppermute(earlier[-1], axis, up))
+    for _ in range((ways - 1) // 2):
+        later.append(lax.ppermute(later[-1], axis, down))
+    line = jnp.concatenate([*earlier[::-1], *later[1:]], axis=dim)
+    return jnp.roll(line, (lax.axis_index(axis) - ways // 2) * array.shape[dim], axis=dim)
 
 
 def prefix_2(value, axis, combine, identity):
@@ -73,7 +86,7 @@
     scale = lax.rsqrt(jnp.mean(mixed * mixed, axis=-1, keepdims=True) + epsilon)
     normed = (mixed * scale * norm_gain.reshape(1, heads, 1, head_size)).astype(jnp.bfloat16)
     normed = normed.transpose(0, 2, 1, 3).reshape(requests * block, width_here)
-    all_heads = lax.all_gather(normed, "tensor", axis=1, tiled=True)
+    all_heads = gather_around(normed, "tensor", 1)
     projected = jnp.dot(
         all_heads,
         lax.all_gather(out_weight, "context", axis=0, tiled=True),

time: 249 us -> 236 us (0.948)
  the two profiles are of different devices: /device:TPU:1 before, /device:TPU:16 now
where the time goes in v1:
time: 236 us; the launch traced here: 234 us
  waiting for transfers between devices  84.8 us (36%)
  local copies, waits for them, and re-layouts  36.2 us (15%)
  blocking collectives  35.8 us (15%)
  other arithmetic  32.3 us (14%)
  starting transfers between devices  22 us (9%)
  between operations  13.5 us (6%)
  matrix products  8.97 us (4%)
    all_gather x1, waiting for transfers between devices, prefix_2(): lax.all_gather(part.astype(kind), axis)  49.7 us
    all_gather x1, blocking collectives, prefix_2(): lax.all_gather(part.astype(kind), axis)  35.8 us
    ppermute x8, waiting for transfers between devices, gather_around(): earlier.append(lax.ppermute(earlier[-1], axis, up))  33.1 us
    select_n x32, other arithmetic, lap(): return jax.tree.map(lambda a, b: jnp.where(reached, a, b), new, before)  29.7 us
    unnamed x34, local copies, waits for them, and re-layouts  26.2 us
    ppermute x7, starting transfers between devices, gather_around(): later.append(lax.ppermute(later[-1], axis, down))  22 us
    dot_general x1, matrix products, local(): jnp.dot(all_heads, lax.all_gather(out_weight, 'context', axis=0, tiled=Tr...  6.64 us
    dynamic_slice x64, local copies, waits for them, and re-layouts, lap(): part[k].astype(own.dtype)  6.03 us
  transfers between devices with their start and end apart: 17, of which 12 were waited for; matrix products, arithmetic and copies ran while one was open for 28% of the time, Pallas kernels for 0%

profile of v1, /device:TPU:16, one launch (start us, length us, event | category | flops | bytes accessed | tf_op | source)
XLA Modules:
  0.0 234.2 jit_solution(13460801782328462261)
XLA Ops:
  8.4 1.1 multiply_convert_fusion.3
  9.5 1.1 copy.44
  12.6 35.8 %all-gather = bf16[32,2,1]{2,1,0:T(2,128)(2,1)S(1)} all-gather(bf16[1,2,1]{2,1,0:T(2,128)(2,1)S(1)} %get-tuple-element.154), channel_id=2, replica_groups=mesh['context'=32,'tensor'=16] {'context'}, dimensions={0}, use_global_device_ids=true | all-gather | bytes 132 | tf_op jit(solution)/shard_map/all_gather | solution.py:25
  48.5 1.0 fusion.26
  49.5 49.7 %all-gather.7.cloned.1.call-done = bf16[64,128,128]{2,1,0:T(8,128)(2,1)} async-done(((bf16[2,128,128]{2,1,0:T(8,128)(2,1)}), bf16[64,128,128]{2,1,0:T(8,128)(2,1)}) %all-gather.7.cloned.1.call-update) | async-done | bytes 2097168 | tf_op jit(solution)/shard_map/all_gather | solution.py:25
  99.2 36.5 %while.14 = (s32[]{:T(128)}, f32[1,2,128,128]{3,2,1,0:T(8,128)S(1)}, s32[]{:T(128)}, bf16[32,1,2]{0,2,1:T(2,128)(2,1)S(1)}, bf16[32,1,2,128,128]{4,3,2,1,0:T(8,128)(2,1)}, /*index=5*/s32[]{:T(128)}, s32[]{:T(128)}) while((s32[]{:T(128)}, f32[1,2,128,128]{3,2,1,0:T(8,128)S(1)}, s32[]{:T(128)}, bf16[32,1,2]{0,2,1:T(2,128)(2,1)S(1)}, ...), condition=%wide.region_3.4_spmd.clone, body=%wide.region_2.3_spmd.clone.sunk | while | flops 163846 | bytes 327821 | solution.py:42
  107.4 0.9 fusion.34
  108.5 0.9 fusion.34
  114.2 0.9 fusion.34
  115.4 0.9 fusion.34
  131.4 0.9 fusion.34
  136.2 1.0 multiply_reduce_fusion
  137.4 7.0 %collective-permute-done = bf16[512,256]{0,1:T(8,128)(2,1)S(1)} collective-permute-done((bf16[512,256]{0,1:T(8,128)(2,1)S(1)}, bf16[512,256]{0,1:T(8,128)(2,1)S(1)}, u32[]{:S(2)}, u32[]{:S(2)}) %collective-permute-start) | collective-permute-done | bytes 262176 | tf_op jit(solution)/shard_map/ppermute | solution.py:15
  144.4 3.0 %collective-permute-start.8 = (bf16[512,256]{0,1:T(8,128)(2,1)S(1)}, bf16[512,256]{0,1:T(8,128)(2,1)S(1)}, u32[]{:S(2)}, u32[]{:S(2)}) collective-permute-start(bf16[512,256]{0,1:T(8,128)(2,1)S(1)} %bitcast.59), channel_id=1, source_target_pairs={{0,15},{1,0},{2,1},{3,2},{4,3},{5,4},{6,5},{7,6},{8,7},{9,8},{10,9... | collective-permute-start | bytes 786440 | tf_op jit(solution)/shard_map/ppermute | solution.py:17
  147.3 4.1 %collective-permute-done.1 = bf16[512,256]{0,1:T(8,128)(2,1)S(1)} collective-permute-done((bf16[512,256]{0,1:T(8,128)(2,1)S(1)}, bf16[512,256]{0,1:T(8,128)(2,1)S(1)}, u32[]{:S(2)}, u32[]{:S(2)}) %collective-permute-start.1) | collective-permute-done | bytes 262176 | tf_op jit(solution)/shard_map/ppermute | solution.py:15
  151.4 3.0 %collective-permute-start.9 = (bf16[512,256]{0,1:T(8,128)(2,1)S(1)}, bf16[512,256]{0,1:T(8,128)(2,1)S(1)}, u32[]{:S(2)}, u32[]{:S(2)}) collective-permute-start(bf16[512,256]{0,1:T(8,128)(2,1)S(1)} %collective-permute-done.8), channel_id=1, source_target_pairs={{0,15},{1,0},{2,1},{3,2},{4,3},{5,4},{6,5},{7,6},{8,7},{9,8},{10,9... | collective-permute-start | bytes 786440 | tf_op jit(solution)/shard_map/ppermute | solution.py:17
  154.3 4.0 %collective-permute-done.2 = bf16[512,256]{0,1:T(8,128)(2,1)S(1)} collective-permute-done((bf16[512,256]{0,1:T(8,128)(2,1)S(1)}, bf16[512,256]{0,1:T(8,128)(2,1)S(1)}, u32[]{:S(2)}, u32[]{:S(2)}) %collective-permute-start.2) | collective-permute-done | bytes 262176 | tf_op jit(solution)/shard_map/ppermute | solution.py:15
  158.4 3.0 %collective-permute-start.10 = (bf16[512,256]{0,1:T(8,128)(2,1)S(1)}, bf16[512,256]{0,1:T(8,128)(2,1)S(1)}, u32[]{:S(2)}, u32[]{:S(2)}) collective-permute-start(bf16[512,256]{0,1:T(8,128)(2,1)S(1)} %collective-permute-done.9), channel_id=1, source_target_pairs={{0,15},{1,0},{2,1},{3,2},{4,3},{5,4},{6,5},{7,6},{8,7},{9,8},{10,9... | collective-permute-start | bytes 786440 | tf_op jit(solution)/shard_map/ppermute | solution.py:17
  161.3 4.0 %collective-permute-done.3 = bf16[512,256]{0,1:T(8,128)(2,1)S(1)} collective-permute-done((bf16[512,256]{0,1:T(8,128)(2,1)S(1)}, bf16[512,256]{0,1:T(8,128)(2,1)S(1)}, u32[]{:S(2)}, u32[]{:S(2)}) %collective-permute-start.3) | collective-permute-done | bytes 262176 | tf_op jit(solution)/shard_map/ppermute | solution.py:15
  165.4 3.4 %collective-permute-start.11 = (bf16[512,256]{0,1:T(8,128)(2,1)S(1)}, bf16[512,256]{0,1:T(8,128)(2,1)S(1)}, u32[]{:S(2)}, u32[]{:S(2)}) collective-permute-start(bf16[512,256]{0,1:T(8,128)(2,1)S(1)} %collective-permute-done.10), channel_id=1, source_target_pairs={{0,15},{1,0},{2,1},{3,2},{4,3},{5,4},{6,5},{7,6},{8,7},{9,8},{10,9... | collective-permute-start | bytes 786440 | tf_op jit(solution)/shard_map/ppermute | solution.py:17
  168.7 3.6 %collective-permute-done.4 = bf16[512,256]{0,1:T(8,128)(2,1)S(1)} collective-permute-done((bf16[512,256]{0,1:T(8,128)(2,1)S(1)}, bf16[512,256]{0,1:T(8,128)(2,1)S(1)}, u32[]{:S(2)}, u32[]{:S(2)}) %collective-permute-start.4) | collective-permute-done | bytes 262176 | tf_op jit(solution)/shard_map/ppermute | solution.py:15
  172.6 3.5 %collective-permute-start.12 = (bf16[512,256]{0,1:T(8,128)(2,1)S(1)}, bf16[512,256]{0,1:T(8,128)(2,1)S(1)}, u32[]{:S(2)}, u32[]{:S(2)}) collective-permute-start(bf16[512,256]{0,1:T(8,128)(2,1)S(1)} %collective-permute-done.11), channel_id=1, source_target_pairs={{0,15},{1,0},{2,1},{3,2},{4,3},{5,4},{6,5},{7,6},{8,7},{9,8},{10,9... | collective-permute-start | bytes 786440 | tf_op jit(solution)/shard_map/ppermute | solution.py:17
  176.2 3.2 %collective-permute-done.5 = bf16[512,256]{0,1:T(8,128)(2,1)S(1)} collective-permute-done((bf16[512,256]{0,1:T(8,128)(2,1)S(1)}, bf16[512,256]{0,1:T(8,128)(2,1)S(1)}, u32[]{:S(2)}, u32[]{:S(2)}) %collective-permute-start.5) | collective-permute-done | bytes 262176 | tf_op jit(solution)/shard_map/ppermute | solution.py:15
  180.0 3.1 %collective-permute-start.13 = (bf16[512,256]{0,1:T(8,128)(2,1)S(1)}, bf16[512,256]{0,1:T(8,128)(2,1)S(1)}, u32[]{:S(2)}, u32[]{:S(2)}) collective-permute-start(bf16[512,256]{0,1:T(8,128)(2,1)S(1)} %collective-permute-done.12), channel_id=1, source_target_pairs={{0,15},{1,0},{2,1},{3,2},{4,3},{5,4},{6,5},{7,6},{8,7},{9,8},{10,9... | collective-permute-start | bytes 786440 | tf_op jit(solution)/shard_map/ppermute | solution.py:17
  183.2 3.4 %collective-permute-done.6 = bf16[512,256]{0,1:T(8,128)(2,1)} collective-permute-done((bf16[512,256]{0,1:T(8,128)(2,1)S(1)}, bf16[512,256]{0,1:T(8,128)(2,1)}, u32[]{:S(2)}, u32[]{:S(2)}) %collective-permute-start.6) | collective-permute-done | bytes 262176 | tf_op jit(solution)/shard_map/ppermute | solution.py:15
  187.0 3.1 %collective-permute-start.14 = (bf16[512,256]{0,1:T(8,128)(2,1)S(1)}, bf16[512,256]{0,1:T(8,128)(2,1)S(1)}, u32[]{:S(2)}, u32[]{:S(2)}) collective-permute-start(bf16[512,256]{0,1:T(8,128)(2,1)S(1)} %collective-permute-done.13), channel_id=1, source_target_pairs={{0,15},{1,0},{2,1},{3,2},{4,3},{5,4},{6,5},{7,6},{8,7},{9,8},{10,9... | collective-permute-start | bytes 786440 | tf_op jit(solution)/shard_map/ppermute | solution.py:17
  190.2 3.7 %collective-permute-done.7 = bf16[512,256]{0,1:T(8,128)(2,1)} collective-permute-done((bf16[512,256]{0,1:T(8,128)(2,1)}, bf16[512,256]{0,1:T(8,128)(2,1)}, u32[]{:S(2)}, u32[]{:S(2)}) %collective-permute-start.7) | collective-permute-done | bytes 262176 | tf_op jit(solution)/shard_map/ppermute | solution.py:15
  193.8 1.7 constant_dynamic-update-slice_fusion.31
  195.5 1.7 constant_dynamic-update-slice_fusion.30
  207.3 1.7 constant_dynamic-update-slice_fusion.15
  209.0 1.7 constant_dynamic-update-slice_fusion.14
  220.7 6.6 %fusion.10 = bf16[1,512,512]{2,1,0:T(8,128)(2,1)} fusion(bf16[4096,512]{1,0:T(8,128)(2,1)} %all-gather.5.cloned.1.call-done, bf16[512,8192]{0,1:T(8,128)(2,1)} %constant_dynamic-update-slice_fusion, s32[]{:T(128)S(6)} %select_n.42, bf16[1,512,512]{2,1,0:T(8,128)(2,1)} %param.17), kind=kOutput, calls=%fused_computation.10 | convolution fusion | flops 2148270080 | bytes 9437188 | tf_op jit(solution)/shard_map/dot_general | solution.py:90
  (195 shorter events, 57.5 us)
Async XLA Ops:
  6.5 130.7 %copy-start = (f32[256]{0:T(256)S(1)}, f32[256]{0:T(256)}, u32[]{:S(2)}) copy-start(f32[256]{0:T(256)} %param.15) | copy-start | bytes 3076
  6.5 92.7 %all-gather.7.cloned.1.call-start = ((), (), s32[]{:S(2)}) async-start(), calls=%async_computation.1 | async-start | bytes 2162688 | tf_op jit(solution)/shard_map/all_gather | solution.py:25
  11.8 209.0 %all-gather.5.cloned.1.call-start = ((), (), s32[]{:S(2)}) async-start(), calls=%async_computation | async-start | bytes 4325376 | tf_op jit(solution)/shard_map/all_gather | solution.py:92
  137.3 7.0 %collective-permute-start = (bf16[512,256]{0,1:T(8,128)(2,1)S(1)}, bf16[512,256]{0,1:T(8,128)(2,1)S(1)}, u32[]{:S(2)}, u32[]{:S(2)}) collective-permute-start(bf16[512,256]{0,1:T(8,128)(2,1)S(1)} %bitcast.58), channel_id=1, source_target_pairs={{0,1},{1,2},{2,3},{3,4},{4,5},{5,6},{6,7},{7,8},{8,9},{9,10},{10,1... | collective-permute-start | bytes 786440 | tf_op jit(solution)/shard_map/ppermute | solution.py:15
  144.4 7.0 %collective-permute-start.1 = (bf16[512,256]{0,1:T(8,128)(2,1)S(1)}, bf16[512,256]{0,1:T(8,128)(2,1)S(1)}, u32[]{:S(2)}, u32[]{:S(2)}) collective-permute-start(bf16[512,256]{0,1:T(8,128)(2,1)S(1)} %collective-permute-done), channel_id=1, source_target_pairs={{0,1},{1,2},{2,3},{3,4},{4,5},{5,6},{6,7},{7,8},{8,9},{9,10},{10,1... | collective-permute-start | bytes 786440 | tf_op jit(solution)/shard_map/ppermute | solution.py:15
  144.4 7.0 %collective-permute-start.8 = (bf16[512,256]{0,1:T(8,128)(2,1)S(1)}, bf16[512,256]{0,1:T(8,128)(2,1)S(1)}, u32[]{:S(2)}, u32[]{:S(2)}) collective-permute-start(bf16[512,256]{0,1:T(8,128)(2,1)S(1)} %bitcast.59), channel_id=1, source_target_pairs={{0,15},{1,0},{2,1},{3,2},{4,3},{5,4},{6,5},{7,6},{8,7},{9,8},{10,9... | collective-permute-start | bytes 786440 | tf_op jit(solution)/shard_map/ppermute | solution.py:17
  151.4 7.0 %collective-permute-start.2 = (bf16[512,256]{0,1:T(8,128)(2,1)S(1)}, bf16[512,256]{0,1:T(8,128)(2,1)S(1)}, u32[]{:S(2)}, u32[]{:S(2)}) collective-permute-start(bf16[512,256]{0,1:T(8,128)(2,1)S(1)} %collective-permute-done.1), channel_id=1, source_target_pairs={{0,1},{1,2},{2,3},{3,4},{4,5},{5,6},{6,7},{7,8},{8,9},{9,10},{10,1... | collective-permute-start | bytes 786440 | tf_op jit(solution)/shard_map/ppermute | solution.py:15
  151.4 7.0 %collective-permute-start.9 = (bf16[512,256]{0,1:T(8,128)(2,1)S(1)}, bf16[512,256]{0,1:T(8,128)(2,1)S(1)}, u32[]{:S(2)}, u32[]{:S(2)}) collective-permute-start(bf16[512,256]{0,1:T(8,128)(2,1)S(1)} %collective-permute-done.8), channel_id=1, source_target_pairs={{0,15},{1,0},{2,1},{3,2},{4,3},{5,4},{6,5},{7,6},{8,7},{9,8},{10,9... | collective-permute-start | bytes 786440 | tf_op jit(solution)/shard_map/ppermute | solution.py:17
  158.4 7.0 %collective-permute-start.3 = (bf16[512,256]{0,1:T(8,128)(2,1)S(1)}, bf16[512,256]{0,1:T(8,128)(2,1)S(1)}, u32[]{:S(2)}, u32[]{:S(2)}) collective-permute-start(bf16[512,256]{0,1:T(8,128)(2,1)S(1)} %collective-permute-done.2), channel_id=1, source_target_pairs={{0,1},{1,2},{2,3},{3,4},{4,5},{5,6},{6,7},{7,8},{8,9},{9,10},{10,1... | collective-permute-start | bytes 786440 | tf_op jit(solution)/shard_map/ppermute | solution.py:15
  158.4 7.0 %collective-permute-start.10 = (bf16[512,256]{0,1:T(8,128)(2,1)S(1)}, bf16[512,256]{0,1:T(8,128)(2,1)S(1)}, u32[]{:S(2)}, u32[]{:S(2)}) collective-permute-start(bf16[512,256]{0,1:T(8,128)(2,1)S(1)} %collective-permute-done.9), channel_id=1, source_target_pairs={{0,15},{1,0},{2,1},{3,2},{4,3},{5,4},{6,5},{7,6},{8,7},{9,8},{10,9... | collective-permute-start | bytes 786440 | tf_op jit(solution)/shard_map/ppermute | solution.py:17
  165.4 7.0 %collective-permute-start.4 = (bf16[512,256]{0,1:T(8,128)(2,1)S(1)}, bf16[512,256]{0,1:T(8,128)(2,1)S(1)}, u32[]{:S(2)}, u32[]{:S(2)}) collective-permute-start(bf16[512,256]{0,1:T(8,128)(2,1)S(1)} %collective-permute-done.3), channel_id=1, source_target_pairs={{0,1},{1,2},{2,3},{3,4},{4,5},{5,6},{6,7},{7,8},{8,9},{9,10},{10,1... | collective-permute-start | bytes 786440 | tf_op jit(solution)/shard_map/ppermute | solution.py:15
  165.4 7.2 %collective-permute-start.11 = (bf16[512,256]{0,1:T(8,128)(2,1)S(1)}, bf16[512,256]{0,1:T(8,128)(2,1)S(1)}, u32[]{:S(2)}, u32[]{:S(2)}) collective-permute-start(bf16[512,256]{0,1:T(8,128)(2,1)S(1)} %collective-permute-done.10), channel_id=1, source_target_pairs={{0,15},{1,0},{2,1},{3,2},{4,3},{5,4},{6,5},{7,6},{8,7},{9,8},{10,9... | collective-permute-start | bytes 786440 | tf_op jit(solution)/shard_map/ppermute | solution.py:17
  172.4 7.0 %collective-permute-start.5 = (bf16[512,256]{0,1:T(8,128)(2,1)S(1)}, bf16[512,256]{0,1:T(8,128)(2,1)S(1)}, u32[]{:S(2)}, u32[]{:S(2)}) collective-permute-start(bf16[512,256]{0,1:T(8,128)(2,1)S(1)} %collective-permute-done.4), channel_id=1, source_target_pairs={{0,1},{1,2},{2,3},{3,4},{4,5},{5,6},{6,7},{7,8},{8,9},{9,10},{10,1... | collective-permute-start | bytes 786440 | tf_op jit(solution)/shard_map/ppermute | solution.py:15
  172.6 7.4 %collective-permute-start.12 = (bf16[512,256]{0,1:T(8,128)(2,1)S(1)}, bf16[512,256]{0,1:T(8,128)(2,1)S(1)}, u32[]{:S(2)}, u32[]{:S(2)}) collective-permute-start(bf16[512,256]{0,1:T(8,128)(2,1)S(1)} %collective-permute-done.11), channel_id=1, source_target_pairs={{0,15},{1,0},{2,1},{3,2},{4,3},{5,4},{6,5},{7,6},{8,7},{9,8},{10,9... | collective-permute-start | bytes 786440 | tf_op jit(solution)/shard_map/ppermute | solution.py:17
  179.4 7.1 %collective-permute-start.6 = (bf16[512,256]{0,1:T(8,128)(2,1)S(1)}, bf16[512,256]{0,1:T(8,128)(2,1)}, u32[]{:S(2)}, u32[]{:S(2)}) collective-permute-start(bf16[512,256]{0,1:T(8,128)(2,1)S(1)} %collective-permute-done.5), channel_id=1, source_target_pairs={{0,1},{1,2},{2,3},{3,4},{4,5},{5,6},{6,7},{7,8},{8,9},{9,10},{10,1... | collective-permute-start | bytes 786440 | tf_op jit(solution)/shard_map/ppermute | solution.py:15
  180.0 7.0 %collective-permute-start.13 = (bf16[512,256]{0,1:T(8,128)(2,1)S(1)}, bf16[512,256]{0,1:T(8,128)(2,1)S(1)}, u32[]{:S(2)}, u32[]{:S(2)}) collective-permute-start(bf16[512,256]{0,1:T(8,128)(2,1)S(1)} %collective-permute-done.12), channel_id=1, source_target_pairs={{0,15},{1,0},{2,1},{3,2},{4,3},{5,4},{6,5},{7,6},{8,7},{9,8},{10,9... | collective-permute-start | bytes 786440 | tf_op jit(solution)/shard_map/ppermute | solution.py:17
  186.5 7.3 %collective-permute-start.7 = (bf16[512,256]{0,1:T(8,128)(2,1)}, bf16[512,256]{0,1:T(8,128)(2,1)}, u32[]{:S(2)}, u32[]{:S(2)}) collective-permute-start(bf16[512,256]{0,1:T(8,128)(2,1)} %collective-permute-done.6), channel_id=1, source_target_pairs={{0,1},{1,2},{2,3},{3,4},{4,5},{5,6},{6,7},{7,8},{8,9},{9,10},{10,1... | collective-permute-start | bytes 786440 | tf_op jit(solution)/shard_map/ppermute | solution.py:15
  187.0 19.5 %collective-permute-start.14 = (bf16[512,256]{0,1:T(8,128)(2,1)S(1)}, bf16[512,256]{0,1:T(8,128)(2,1)S(1)}, u32[]{:S(2)}, u32[]{:S(2)}) collective-permute-start(bf16[512,256]{0,1:T(8,128)(2,1)S(1)} %collective-permute-done.13), channel_id=1, source_target_pairs={{0,15},{1,0},{2,1},{3,2},{4,3},{5,4},{6,5},{7,6},{8,7},{9,8},{10,9... | collective-permute-start | bytes 786440 | tf_op jit(solution)/shard_map/ppermute | solution.py:17
Sparse Core Ops, SparseCore 0:
  11.9 87.2 all-gather.6
  102.3 83.9 all-gather.4
